TPU v7x, 256 devices: a whole 4x4x8 slice. The times are simulated.
256 devices in a mesh: sq: 8 (over z), ex: 32 (over x, y, core).
Axes of the slice: x: 4, y: 4, z: 8, core: 2. Of those that a mesh axis runs over, the one named last changes fastest.
Arguments:
- tokens: bfloat16 [16384, 2048], P(('sq', 'ex')), may hold values from -6 to 6
- venue_id: int32 [16384], P(('sq', 'ex')), may hold values from 0 to 15
- time_rank: int32 [16384], replicated, may hold values from 0 to 16383, each once
- routes: int32 [16384, 6], P(('sq', 'ex')), may hold values from 0 to 31, all different within a row; in each aligned block of 64 rows (0 to 63, 64 to 127, ...) at most 30 rows name the same one
- venue_table: bfloat16 [16, 2048], replicated, may hold values from -3 to 3
- attn_gain: float32 [2048], replicated, may hold values from 0.8 to 8
- w_qkv: bfloat16 [2048, 3, 1024], P(None, None, 'sq'), may hold values from -0.125 to 0.125
- w_out: bfloat16 [1024, 2048], P('sq'), may hold values from -0.5 to 0.5
- ffn_gain: float32 [2048], replicated, may hold values from 0.5 to 1.5
- router: bfloat16 [2048, 32], replicated, may hold values from -0.125 to 0.125
- expert_in: bfloat16 [32, 2, 2048, 768], P('ex'), may hold values from -0.125 to 0.125
- expert_out: bfloat16 [32, 768, 2048], P('ex'), may hold values from -0.21875 to 0.21875
Outputs:
- attended: bfloat16 [16384, 2048], P(('sq', 'ex'))
- layer_out: bfloat16 [16384, 2048], P(('sq', 'ex'))
Inputs may be any that keep to these rules, and one draw needn't show every extreme that they name: `routes`: each token names 6 different experts; among the 64 rows of one device no expert is named by more than 30 rows, and in every draw some expert is named by exactly 30 rows of some device. `time_rank`: each of 0 to 16383 appears once.
All inputs are finite; a program needn't handle non-finite values.
Results may differ from a plain program's by a relative error of at most 0.019.
The roundings to bfloat16 on the way count: a program that leaves them out, or rounds other values in their place, can miss the bound.
Values may be sent and summed in bfloat16 or wider, within the bound.
No kernel may reach another device: no remote copies, remote signals or barrier semaphores. Data moves between devices by JAX's collectives and lax.ppermute only.
A program may use at most 128 MiB of HBM per device.

v0:
```python
import math

import jax
import jax.numpy as jnp
from jax import lax
from jax.sharding import PartitionSpec as P

epsilon = 1e-06
neg_large = -1e30


def rms_norm(values, gain):
    mean_square = jnp.mean(values * values, axis=-1, keepdims=True)
    return values * lax.rsqrt(mean_square + epsilon) * gain


def rank_rows(time_rank, first_row, row_count, group_rows, tok_rows, ex_count):
    row_ids = first_row + jnp.arange(row_count, dtype=jnp.int32)
    owner_index = row_ids // group_rows
    within = row_ids % group_rows
    global_row = (within // tok_rows * ex_count + owner_index) * tok_rows + within % tok_rows
    return jnp.take(time_rank, global_row)


def online_block(carry_state, query_block, query_rank, key_block, value_block, key_rank, inv_scale):
    row_best, row_total, accumulated = carry_state
    scores = (
        lax.dot_general(
            query_block, key_block, (((1,), (1,)), ((), ())), preferred_element_type=jnp.float32
        )
        * inv_scale
    )
    allowed = key_rank[None, :] <= query_rank[:, None]
    masked = jnp.where(allowed, scores, neg_large)
    new_best = jnp.maximum(row_best, jnp.max(masked, axis=1))
    probs = jnp.where(allowed, jnp.exp(masked - new_best[:, None]), 0.0)
    factor = jnp.exp(row_best - new_best)
    row_total = row_total * factor + jnp.sum(probs, axis=1)
    accumulated = accumulated * factor[:, None] + jnp.dot(
        probs.astype(jnp.bfloat16), value_block, preferred_element_type=jnp.float32
    )
    return (new_best, row_total, accumulated)


def empty_state(row_count, head_dim):
    return (
        jnp.full((row_count,), neg_large, jnp.float32),
        jnp.zeros((row_count,), jnp.float32),
        jnp.zeros((row_count, head_dim), jnp.float32),
    )


def body(
    tokens,
    venue_id,
    time_rank,
    routes,
    venue_table,
    attn_gain,
    w_qkv,
    w_out,
    ffn_gain,
    router,
    expert_in,
    expert_out,
):
    tok_rows, model_width = tokens.shape
    head_dim = w_out.shape[0]
    sq_count = lax.axis_size("sq")
    ex_count = lax.axis_size("ex")
    ex_index = lax.axis_index("ex")
    inv_scale = 1.0 / math.sqrt(head_dim)
    venue_hot = (
        venue_id[:, None] == jnp.arange(venue_table.shape[0], dtype=jnp.int32)[None, :]
    ).astype(jnp.bfloat16)
    base_rows = tokens.astype(jnp.float32) + jnp.dot(
        venue_hot, venue_table, preferred_element_type=jnp.float32
    )
    normed = rms_norm(base_rows, attn_gain).astype(jnp.bfloat16)
    flat_qkv = w_qkv.reshape(model_width, 3 * head_dim)
    projected = jnp.dot(
        lax.all_gather(normed, "sq", axis=0, tiled=True),
        flat_qkv,
        preferred_element_type=jnp.float32,
    ).astype(jnp.bfloat16)
    group_rows = projected.shape[0]
    queries = projected[:, :head_dim]
    key_rows = projected[:, head_dim : 2 * head_dim]
    value_rows = projected[:, 2 * head_dim :]
    query_rank = rank_rows(
        time_rank, ex_index * group_rows, group_rows, group_rows, tok_rows, ex_count
    )
    carry_state = empty_state(group_rows, head_dim)
    shard_piece = (
        lax.all_gather(key_rows, "ex", axis=0, tiled=True),
        lax.all_gather(value_rows, "ex", axis=0, tiled=True),
    )
    row_count = shard_piece[0].shape[0]
    block_size = math.gcd(row_count, 1024)
    block_count = row_count // block_size
    piece_rank = rank_rows(time_rank, jnp.int32(0), row_count, group_rows, tok_rows, ex_count)
    stacked = (
        shard_piece[0].reshape(block_count, block_size, head_dim),
        shard_piece[1].reshape(block_count, block_size, head_dim),
        piece_rank.reshape(block_count, block_size),
    )

    def step_block(state, items):
        return (
            online_block(state, queries, query_rank, items[0], items[1], items[2], inv_scale),
            None,
        )

    carry_state, unused = lax.scan(step_block, carry_state, stacked)
    row_best, row_total, accumulated = carry_state
    head_out = (accumulated / row_total[:, None]).astype(jnp.bfloat16)
    regrouped = lax.all_to_all(head_out, "sq", split_axis=0, concat_axis=1, tiled=True)
    all_out = lax.all_gather(w_out, "sq", axis=0, tiled=True)
    per_head = jnp.einsum(
        "thd,hde->hte",
        regrouped.reshape(tok_rows, sq_count, head_dim),
        all_out.reshape(sq_count, head_dim, model_width),
        preferred_element_type=jnp.float32,
    ).astype(jnp.bfloat16)
    attn_sum = jnp.sum(per_head.astype(jnp.float32), axis=0)
    hidden_state = base_rows + attn_sum
    normed_ffn = rms_norm(hidden_state, ffn_gain).astype(jnp.bfloat16)
    logits = jnp.dot(normed_ffn, router, preferred_element_type=jnp.float32)
    expert_count = router.shape[1]
    top_count = routes.shape[1]
    route_hot = routes[:, :, None] == jnp.arange(expert_count, dtype=jnp.int32)[None, None, :]
    chosen = jnp.sum(jnp.where(route_hot, logits[:, None, :], 0.0), axis=2)
    raw_gate = jax.nn.sigmoid(chosen)
    gate_weights = raw_gate / jnp.sum(raw_gate, axis=1, keepdims=True)
    capacity = min(tok_rows, tok_rows * top_count * 5 // (2 * expert_count))
    pair_hot = route_hot.reshape(tok_rows * top_count, expert_count).astype(jnp.int32)
    earlier = jnp.cumsum(pair_hot, axis=0) - pair_hot
    slot_index = jnp.sum(earlier * pair_hot, axis=1)
    target_slot = routes.reshape(-1) * capacity + slot_index
    pair_token = jnp.arange(tok_rows * top_count, dtype=jnp.int32) // top_count
    outgoing = (
        jnp.zeros((expert_count * capacity, model_width), jnp.bfloat16)
        .at[target_slot]
        .set(normed_ffn[pair_token])
    )
    outgoing = outgoing.reshape(expert_count, capacity, model_width)
    local_experts = expert_in.shape[0]
    arrived = lax.all_to_all(outgoing, "ex", split_axis=0, concat_axis=0, tiled=True)
    slot_count = arrived.shape[1]
    grouped = arrived.reshape(ex_count, local_experts, slot_count, model_width)
    gate_part = jnp.einsum(
        "sekd,edf->sekf", grouped, expert_in[:, 0], preferred_element_type=jnp.float32
    )
    up_part = jnp.einsum(
        "sekd,edf->sekf", grouped, expert_in[:, 1], preferred_element_type=jnp.float32
    )
    hidden = (jax.nn.silu(gate_part) * up_part).astype(jnp.bfloat16)
    produced = jnp.einsum(
        "sekf,efd->sekd", hidden, expert_out, preferred_element_type=jnp.float32
    ).astype(jnp.bfloat16)
    returned = lax.all_to_all(
        produced.reshape(ex_count * local_experts, slot_count, model_width),
        "ex",
        split_axis=0,
        concat_axis=0,
        tiled=True,
    )
    gathered_rows = returned.reshape(expert_count * capacity, model_width)[target_slot]
    gathered_rows = gathered_rows.reshape(tok_rows, top_count, model_width)
    moe_sum = jnp.sum(gate_weights[:, :, None] * gathered_rows.astype(jnp.float32), axis=1)
    attended = attn_sum.astype(jnp.bfloat16)
    layer_out = (hidden_state + moe_sum).astype(jnp.bfloat16)
    return (attended, layer_out)


def solution(mesh):
    placed = (
        P(("sq", "ex"), None),
        P(("sq", "ex")),
        P(),
        P(("sq", "ex"), None),
        P(),
        P(),
        P(None, None, "sq"),
        P("sq", None),
        P(),
        P(),
        P("ex", None, None, None),
        P("ex", None, None),
    )
    return jax.shard_map(
        body,
        mesh=mesh,
        in_specs=placed,
        out_specs=(P(("sq", "ex"), None), P(("sq", "ex"), None)),
        check_vma=False,
    )
```

profile of v0, /device:TPU:8, one launch (start us, length us, event | category | flops | bytes accessed | tf_op | source)
XLA Modules:
  0.0 508.6 jit_solution(10208727239930789802)
XLA Ops:
  13.8 41.4 %all-gather.5.cloned.1.call-done = bf16[512,2048]{1,0:T(8,128)(2,1)} async-done(((bf16[64,2048]{1,0:T(8,128)(2,1)}), bf16[512,2048]{1,0:T(8,128)(2,1)}) %all-gather.5.cloned.1.call-update) | async-done | bytes 2097168 | tf_op jit(solution)/shard_map/all_gather | solution.py:82
  55.3 3.3 convolution_convert_fusion.2
  64.4 90.5 %gather_fusion = s32[16384]{0:T(1024)S(1)} fusion(s32[16384]{0:T(1024)S(1)} %copy-done.1, s32[16384]{0:T(1024)S(1)} %broadcast_clamp_fusion), kind=kCustom, calls=%fused_computation | custom fusion | bytes 196608 | tf_op jit(solution)/shard_map/jit(_take)/gather | solution.py:22
  156.4 6.2 %all-gather.9.cloned.1.call-done = bf16[16384,128]{1,0:T(8,128)(2,1)} async-done(((bf16[512,128]{1,0:T(8,128)(2,1)}), bf16[16384,128]{1,0:T(8,128)(2,1)}) %all-gather.9.cloned.1.call-update) | async-done | bytes 4194320 | tf_op jit(solution)/shard_map/all_gather | solution.py:96
  162.6 133.2 %while.15 = (s32[]{:T(128)}, f32[512]{0:T(512)S(1)}, f32[512]{0:T(512)S(1)}, f32[512,128]{1,0:T(8,128)}, s32[16,1024]{1,0:T(8,128)S(1)}, /*index=5*/s32[512]{0:T...) while((s32[]{:T(128)}, f32[512]{0:T(512)S(1)}, ...), condition=%wide.region_4.5_spmd.clone, body=%wide.region_1.4_spmd.clone.sunk | while | flops 277023232 | bytes 7531645 | solution.py:114
  175.9 3.3 convolution_add_fusion.3
  184.2 3.3 convolution_add_fusion.3
  192.6 3.3 convolution_add_fusion.3
  200.9 3.3 convolution_add_fusion.3
  209.3 3.3 convolution_add_fusion.3
  217.6 3.3 convolution_add_fusion.3
  226.0 3.3 convolution_add_fusion.3
  234.3 3.3 convolution_add_fusion.3
  242.6 3.3 convolution_add_fusion.3
  250.9 3.3 convolution_add_fusion.3
  267.6 3.3 convolution_add_fusion.3
  275.9 3.3 convolution_add_fusion.3
  284.2 3.3 convolution_add_fusion.3
  297.6 7.0 %all-to-all-start = ((bf16[8,64,128]{2,1,0:T(8,128)(2,1)}), bf16[8,64,128]{2,1,0:T(8,128)(2,1)S(1)}, u32[]{:S(2)}, u32[]{:S(2)}) async-start(bf16[8,64,128]{2,1,0:T(8,128)(2,1)} %bitcast.5), calls=%async_computation | async-start | bytes 262144 | tf_op jit(solution)/shard_map/all_to_all | solution.py:117
  305.1 9.1 %all-to-all-done = bf16[8,64,128]{2,1,0:T(8,128)(2,1)S(1)} async-done(((bf16[8,64,128]{2,1,0:T(8,128)(2,1)}), bf16[8,64,128]{2,1,0:T(8,128)(2,1)S(1)}, u32[]{:S(2)}, u32[]{:S(2)}) %all-to-all-start) | async-done | bytes 131104 | tf_op jit(solution)/shard_map/all_to_all | solution.py:117
  319.0 10.3 %scatter_custom_fusion = bf16[960,2048]{1,0:T(8,128)(2,1)} fusion(s32[384]{0:T(512)S(1)} %fusion.79, bf16[]{:T(256)} %constant.184.clone.1, bf16[64,2048]{1,0:T(8,128)(2,1)S(1)} %multiply_convert_fusion, s32[1024]{0:T(1024)S(1)} %pad_clamp_fusion.1), kind=kCustom, calls=%fused_computation.53 | custom fusion | bytes 3932162 | tf_op jit(solution)/shard_map/scatter | solution.py:144
  329.4 5.0 reshape.504
  334.4 55.3 %all_to_all.26 = bf16[32,30,2048]{2,1,0:T(8,128)(2,1)S(1)} all-to-all(bf16[32,30,2048]{2,1,0:T(8,128)(2,1)} %reshape.504), channel_id=1, replica_groups=mesh['sq'=8,'ex'=32] {'ex'}, dimensions={0} | all-to-all | bytes 7864320 | tf_op jit(solution)/shard_map/all_to_all | solution.py:148
  391.6 8.8 %fusion.22 = f32[32,30,768]{2,0,1:T(8,128)} fusion(bf16[32,30,2048]{2,1,0:T(8,128)(2,1)S(1)} %all_to_all.26, bf16[1,2,2048,768]{3,2,1,0:T(8,128)(2,1)} %param.24), kind=kOutput, calls=%fused_computation.37 | convolution fusion | flops 3019898880 | bytes 10027008 | tf_op jit(solution)/shard_map/sekd,edf->sekf/dot_general | solution.py:151
  400.4 13.2 %convolution_convert_fusion = bf16[32,30,2048]{2,0,1:T(8,128)(2,1)} fusion(bf16[1,768,2048]{2,1,0:T(8,128)(2,1)S(1)} %copy-done, f32[32,30,768]{2,0,1:T(8,128)} %fusion.22, bf16[1,2,2048,768]{3,2,1,0:T(8,128)(2,1)} %param.24, bf16[32,30,2048]{2,1,0:T(8,128)(2,1)} %copy-done.6), kind=kOutput, calls=%fused_computation.34 | convolution fusion | flops 6046187520 | bytes 17367040 | tf_op jit(solution)/shard_map/sekf,efd->sekd/dot_general | solution.py:158
  413.6 6.2 %copy.43 = bf16[32,30,2048]{2,1,0:T(8,128)(2,1)} copy(bf16[32,30,2048]{2,0,1:T(8,128)(2,1)} %convolution_convert_fusion) | data formatting | bytes 7864320 | tf_op jit(solution)/shard_map/convert_element_type | solution.py:160
  419.8 6.1 %all-to-all-start.2 = ((bf16[32,30,2048]{2,1,0:T(8,128)(2,1)}), bf16[32,30,2048]{2,1,0:T(8,128)(2,1)}, u32[]{:S(2)}, u32[]{:S(2)}) async-start(bf16[32,30,2048]{2,1,0:T(8,128)(2,1)} %copy.43), calls=%async_computation.2 | async-start | bytes 8388608 | tf_op jit(solution)/shard_map/all_to_all | solution.py:161
  426.3 54.6 %all-to-all-done.2 = bf16[32,30,2048]{2,1,0:T(8,128)(2,1)} async-done(((bf16[32,30,2048]{2,1,0:T(8,128)(2,1)}), bf16[32,30,2048]{2,1,0:T(8,128)(2,1)}, u32[]{:S(2)}, u32[]{:S(2)}) %all-to-all-start.2) | async-done | bytes 3932192 | tf_op jit(solution)/shard_map/all_to_all | solution.py:161
  480.9 5.0 reshape.509
  485.9 7.7 %gather_fusion.2 = bf16[384,2048]{1,0:T(8,128)(2,1)} fusion(bf16[960,2048]{1,0:T(8,128)(2,1)} %reshape.509, s32[1024]{0:T(1024)S(1)} %pad_clamp_fusion), kind=kCustom, calls=%fused_computation.3 | custom fusion | bytes 3147264 | tf_op jit(solution)/shard_map/gather | solution.py:168
  493.6 3.9 reshape.510
  497.5 3.8 multiply_reduce_fusion
  (171 shorter events, 114.3 us)
Async XLA Ops:
  7.2 393.3 %copy-start = (bf16[1,768,2048]{2,1,0:T(8,128)(2,1)S(1)}, bf16[1,768,2048]{2,1,0:T(8,128)(2,1)}, u32[]{:S(2)}) copy-start(bf16[1,768,2048]{2,1,0:T(8,128)(2,1)} %param.25) | copy-start | bytes 9437188
  7.2 48.1 %all-gather.5.cloned.1.call-start = ((), (), s32[]{:S(2)}) async-start(), calls=%async_computation.3 | async-start | bytes 2359296 | tf_op jit(solution)/shard_map/all_gather | solution.py:82
  8.8 0.8 copy-start.2
  11.1 145.3 %all-gather.7.cloned.1.call-start = ((), (), s32[]{:S(2)}) async-start(), calls=%async_computation.4 | async-start | bytes 4325376 | tf_op jit(solution)/shard_map/all_gather | solution.py:95
  55.3 5.7 %copy-start.8 = (s32[64,6]{0,1:T(8,128)S(1)}, s32[64,6]{0,1:T(8,128)}, u32[]{:S(2)}) copy-start(s32[64,6]{0,1:T(8,128)} %param.17) | copy-start | bytes 4612
  58.6 2.6 copy-start.1
  59.4 103.2 %all-gather.9.cloned.1.call-start = ((), (), s32[]{:S(2)}) async-start(), calls=%async_computation.5 | async-start | bytes 4325376 | tf_op jit(solution)/shard_map/all_gather | solution.py:96
  60.1 245.0 %all-gather.11.cloned.1.call-start = ((), (), s32[]{:S(2)}) async-start(), calls=%async_computation.6 | async-start | bytes 4718592 | tf_op jit(solution)/shard_map/all_gather | solution.py:118
  297.6 16.6 %all-to-all-start = ((bf16[8,64,128]{2,1,0:T(8,128)(2,1)}), bf16[8,64,128]{2,1,0:T(8,128)(2,1)S(1)}, u32[]{:S(2)}, u32[]{:S(2)}) async-start(bf16[8,64,128]{2,1,0:T(8,128)(2,1)} %bitcast.5), calls=%async_computation | async-start | bytes 262144 | tf_op jit(solution)/shard_map/all_to_all | solution.py:117
  314.2 3.0 copy-start.3
  314.2 4.7 copy-start.9
  318.1 0.8 copy-start.4
  389.7 1.9 copy-start.6
  419.8 6.1 %copy-start.7 = (bf16[2048,32]{0,1:T(8,128)(2,1)S(1)}, bf16[2048,32]{0,1:T(8,128)(2,1)}, u32[]{:S(2)}) copy-start(bf16[2048,32]{0,1:T(8,128)(2,1)} %param.23) | copy-start | bytes 393220
  419.8 61.1 %all-to-all-start.2 = ((bf16[32,30,2048]{2,1,0:T(8,128)(2,1)}), bf16[32,30,2048]{2,1,0:T(8,128)(2,1)}, u32[]{:S(2)}, u32[]{:S(2)}) async-start(bf16[32,30,2048]{2,1,0:T(8,128)(2,1)} %copy.43), calls=%async_computation.2 | async-start | bytes 8388608 | tf_op jit(solution)/shard_map/all_to_all | solution.py:161
  497.5 3.8 copy-start.5
Sparse Core Ops, SparseCore 0:
  11.2 43.9 all-gather.4
  59.5 49.2 all-gather.6
  112.0 50.5 all-gather.8
  164.2 54.5 all-gather.10
where the time goes:
time: 511 us; the launch traced here: 509 us
  local copies, waits for them, and re-layouts  140 us (27%)
  matrix products  127 us (25%)
  waiting for transfers between devices  113 us (22%)
  blocking collectives  55.3 us (11%)
  other arithmetic  46.3 us (9%)
  between operations  14 us (3%)
  starting transfers between devices  13.2 us (3%)
    gather x3, local copies, waits for them, and re-layouts, rank_rows(): return jnp.take(time_rank, global_row)  93.7 us
    all_to_all x1, blocking collectives, body(): lax.all_to_all(outgoing, 'ex', split_axis=0, concat_axis=0, tiled=True)  55.3 us
    all_to_all x1, waiting for transfers between devices, body(): lax.all_to_all(produced.reshape(ex_count * local_experts, slot_count, mod...  54.6 us
    dot_general x16, matrix products, online_block(): jnp.dot(probs.astype(jnp.bfloat16), value_block, preferred_element_type=j...  52.4 us
    dot_general x16, matrix products, online_block(): lax.dot_general(query_block, key_block, (((1,), (1,)), ((), ())), preferr...  44.7 us
    all_gather x1, waiting for transfers between devices, body(): lax.all_gather(normed, 'sq', axis=0, tiled=True)  41.4 us
    reduce_sum x16, other arithmetic, online_block(): row_total = row_total * factor + jnp.sum(probs, axis=1)  35.4 us
    dot_general x1, matrix products, body(): jnp.einsum('sekf,efd->sekd', hidden, expert_out, preferred_element_type=j...  13.2 us
  transfers between devices with their start and end apart: 6, of which 4 were waited for; matrix products, arithmetic and copies ran while one was open for 46% of the time, Pallas kernels for 0%

commit v1 on v0

v1 whole, which is shorter than its diff:
```python
import functools
import math

import jax
import jax.numpy as jnp
from jax import lax
from jax.experimental import pallas as pl
from jax.experimental.pallas import tpu as pltpu
from jax.sharding import PartitionSpec as P

epsilon = 1e-06
neg_large = -1e30


def rms_norm(values, gain):
    mean_square = jnp.mean(values * values, axis=-1, keepdims=True)
    return values * lax.rsqrt(mean_square + epsilon) * gain


def flash_kernel(key_step, scale, query_ref, keyval_ref, query_rank_ref, key_rank_ref, state_ref, out_ref):
    head_dim = query_ref.shape[1]
    queries = query_ref[...]
    query_count = queries.shape[0]
    query_rank = query_rank_ref[...]
    out_ref[...] = state_ref[...]

    def step(j, carry):
        row_best, row_total = carry
        start = pl.multiple_of(j * key_step, key_step)
        keys = keyval_ref[pl.ds(start, key_step), :head_dim]
        values = keyval_ref[pl.ds(start, key_step), head_dim:]
        scores = lax.dot_general(
            keys, queries, (((1,), (1,)), ((), ())), preferred_element_type=jnp.float32
        )
        key_rank = key_rank_ref[pl.ds(start, key_step), :]
        key_rank = jnp.concatenate([key_rank] * (query_count // 128), axis=1)
        scores = jnp.where(key_rank <= query_rank, scores, neg_large)
        new_best = jnp.maximum(row_best, jnp.max(scores, axis=0, keepdims=True))
        probs = jnp.exp2((scores - new_best) * scale)
        factor = jnp.exp2((row_best - new_best) * scale)
        row_total = row_total * factor + jnp.sum(probs, axis=0, keepdims=True)
        update = lax.dot_general(
            values,
            probs.astype(jnp.bfloat16),
            (((0,), (0,)), ((), ())),
            preferred_element_type=jnp.float32,
        )
        out_ref[:head_dim] = out_ref[:head_dim] * factor + update
        return new_best, row_total

    carry = (state_ref[head_dim : head_dim + 1], state_ref[head_dim + 4 : head_dim + 5])
    best, total = lax.fori_loop(0, keyval_ref.shape[0] // key_step, step, carry)
    out_ref[head_dim:] = jnp.concatenate(
        [jnp.broadcast_to(best, (4, query_count)), jnp.broadcast_to(total, (4, query_count))],
        axis=0,
    )


def flash_part(queries, keyval, query_rank, key_rank, state):
    head_dim = queries.shape[1]
    scale = math.log2(math.e) / math.sqrt(head_dim)
    wide_rank = jnp.broadcast_to(key_rank[:, None], (key_rank.shape[0], 128))
    return pl.pallas_call(
        functools.partial(flash_kernel, 1024, scale),
        out_shape=jax.ShapeDtypeStruct(state.shape, jnp.float32),
        name="flash_part",
        compiler_params=pltpu.CompilerParams(vmem_limit_bytes=48 << 20),
    )(queries, keyval, query_rank[None, :], wide_rank, state)


side = 4
cores = 2
hops = (0, 1, 3, 2)


def ex_id(x, y, c):
    return (x % side) * side * cores + (y % side) * cores + c


def plane_shift(array, amount, first):
    pairs = []
    for x in range(side):
        for y in range(side):
            for c in range(cores):
                if (c == 0) == first:
                    target = ex_id(x + amount, y, c)
                else:
                    target = ex_id(x, y + amount, c)
                pairs.append((ex_id(x, y, c), target))
    return lax.ppermute(array, "ex", pairs)


def plane_gather(array):
    line = jnp.concatenate(
        [array] + [plane_shift(array, s, True) for s in hops[1:]], axis=0
    )
    return jnp.concatenate([line] + [plane_shift(line, s, False) for s in hops[1:]], axis=0)


def plane_sources(ex_index, core):
    x = ex_index // (side * cores)
    y = ex_index // cores % side
    second = jnp.repeat(jnp.array(hops, jnp.int32), side)
    first = jnp.tile(jnp.array(hops, jnp.int32), side)
    shift_x = jnp.where(core == 0, first, second)
    shift_y = jnp.where(core == 0, second, first)
    return (x - shift_x) % side * side * cores + (y - shift_y) % side * cores + core


def core_swap(array):
    return lax.ppermute(array, "ex", [(i, i ^ 1) for i in range(side * side * cores)])


def ring_shift(array, amount):
    count = lax.axis_size("sq")
    return lax.ppermute(array, "sq", [(i, (i + amount) % count) for i in range(count)])


def ring_gather(array):
    half = array.shape[0] // 2
    p1 = ring_shift(array, 1)
    m1 = ring_shift(array, -1)
    p2 = ring_shift(array, 2)
    m2 = ring_shift(array, -2)
    p3 = ring_shift(p2, 1)
    m3 = ring_shift(m2, -1)
    p4 = ring_shift(p2[:half], 2)
    m4 = ring_shift(m2[half:], -2)
    return jnp.concatenate([p3, p2, p1, array, m1, m2, m3, p4, m4], axis=0)


def body(
    tokens,
    venue_id,
    time_rank,
    routes,
    venue_table,
    attn_gain,
    w_qkv,
    w_out,
    ffn_gain,
    router,
    expert_in,
    expert_out,
):
    tok_rows, model_width = tokens.shape
    head_dim = w_out.shape[0]
    sq_count = lax.axis_size("sq")
    ex_count = lax.axis_size("ex")
    ex_index = lax.axis_index("ex")
    venue_hot = (
        venue_id[:, None] == jnp.arange(venue_table.shape[0], dtype=jnp.int32)[None, :]
    ).astype(jnp.bfloat16)
    base_rows = tokens.astype(jnp.float32) + jnp.dot(
        venue_hot, venue_table, preferred_element_type=jnp.float32
    )
    normed = rms_norm(base_rows, attn_gain).astype(jnp.bfloat16)
    flat_qkv = w_qkv.reshape(model_width, 3 * head_dim)
    sq_index = lax.axis_index("sq")
    stream = ring_gather(normed)
    stream, w_out = lax.optimization_barrier((stream, w_out))
    rolled = jnp.dot(stream, flat_qkv, preferred_element_type=jnp.float32).astype(jnp.bfloat16)
    group_rows = rolled.shape[0]
    projected = lax.dynamic_slice_in_dim(
        jnp.concatenate([rolled, rolled], axis=0),
        (3 - sq_index) % sq_count * tok_rows,
        group_rows,
        axis=0,
    )
    queries = projected[:, :head_dim]
    keyval = projected[:, head_dim:]
    ranks = time_rank.reshape(sq_count, ex_count, tok_rows).transpose(1, 0, 2)
    ranks = ranks.reshape(ex_count, group_rows)
    core = ex_index % cores
    query_rank = lax.dynamic_index_in_dim(ranks, ex_index, 0, keepdims=False)
    near_rank = jnp.take(ranks, plane_sources(ex_index, core), axis=0, mode="clip").reshape(-1)
    far_rank = jnp.take(ranks, plane_sources(ex_index, 1 - core), axis=0, mode="clip").reshape(-1)
    near = plane_gather(keyval)
    far = core_swap(near)
    state = jnp.concatenate(
        [
            jnp.zeros((head_dim, group_rows), jnp.float32),
            jnp.full((4, group_rows), neg_large, jnp.float32),
            jnp.zeros((4, group_rows), jnp.float32),
        ],
        axis=0,
    )
    state = flash_part(queries, near, query_rank, near_rank, state)
    state = flash_part(queries, far, query_rank, far_rank, state)
    head_out = (state[:head_dim] / state[head_dim + 4 : head_dim + 5]).T.astype(jnp.bfloat16)
    regrouped = lax.all_to_all(head_out, "sq", split_axis=0, concat_axis=1, tiled=True)
    all_out = lax.all_gather(w_out, "sq", axis=0, tiled=True)
    per_head = jnp.einsum(
        "thd,hde->hte",
        regrouped.reshape(tok_rows, sq_count, head_dim),
        all_out.reshape(sq_count, head_dim, model_width),
        preferred_element_type=jnp.float32,
    ).astype(jnp.bfloat16)
    attn_sum = jnp.sum(per_head.astype(jnp.float32), axis=0)
    hidden_state = base_rows + attn_sum
    normed_ffn = rms_norm(hidden_state, ffn_gain).astype(jnp.bfloat16)
    logits = jnp.dot(normed_ffn, router, preferred_element_type=jnp.float32)
    expert_count = router.shape[1]
    top_count = routes.shape[1]
    expert_ids = jnp.arange(expert_count, dtype=jnp.int32)
    hot = jnp.any(routes[:, :, None] == expert_ids[None, None, :], axis=1)
    raw_gate = jnp.where(hot, jax.nn.sigmoid(logits), 0.0)
    gate_weights = raw_gate / jnp.sum(raw_gate, axis=1, keepdims=True)
    capacity = min(tok_rows, tok_rows * top_count * 5 // (2 * expert_count))
    capacity = -(-capacity // 16) * 16
    hot_count = hot.astype(jnp.int32)
    slot = jnp.cumsum(hot_count, axis=0) - hot_count
    slot = jnp.where(hot, slot, -1)
    taken = slot.T[:, None, :] == jnp.arange(capacity, dtype=jnp.int32)[None, :, None]
    pick = taken.astype(jnp.bfloat16).reshape(expert_count * capacity, tok_rows)
    outgoing = jnp.dot(pick, normed_ffn, preferred_element_type=jnp.float32).astype(jnp.bfloat16)
    outgoing = outgoing.reshape(expert_count, capacity, model_width)
    local_experts = expert_in.shape[0]
    arrived = lax.all_to_all(outgoing, "ex", split_axis=0, concat_axis=0, tiled=True)
    slot_count = arrived.shape[1]
    grouped = arrived.reshape(ex_count, local_experts, slot_count, model_width)
    gate_part = jnp.einsum(
        "sekd,edf->sekf", grouped, expert_in[:, 0], preferred_element_type=jnp.float32
    )
    up_part = jnp.einsum(
        "sekd,edf->sekf", grouped, expert_in[:, 1], preferred_element_type=jnp.float32
    )
    hidden = (jax.nn.silu(gate_part) * up_part).astype(jnp.bfloat16)
    produced = jnp.einsum(
        "sekf,efd->sekd", hidden, expert_out, preferred_element_type=jnp.float32
    ).astype(jnp.bfloat16)
    returned = lax.all_to_all(
        produced.reshape(ex_count * local_experts, slot_count, model_width),
        "ex",
        split_axis=0,
        concat_axis=0,
        tiled=True,
    )
    spread = jnp.where(
        slot[:, :, None] == jnp.arange(capacity, dtype=jnp.int32)[None, None, :],
        gate_weights[:, :, None],
        0.0,
    ).reshape(tok_rows, expert_count * capacity)
    coarse = spread.astype(jnp.bfloat16)
    fine = (spread - coarse.astype(jnp.float32)).astype(jnp.bfloat16)
    both = jnp.dot(
        jnp.concatenate([coarse, fine], axis=0),
        returned.reshape(expert_count * capacity, model_width),
        preferred_element_type=jnp.float32,
    )
    moe_sum = both[:tok_rows] + both[tok_rows:]
    attended = attn_sum.astype(jnp.bfloat16)
    layer_out = (hidden_state + moe_sum).astype(jnp.bfloat16)
    return (attended, layer_out)


def solution(mesh):
    placed = (
        P(("sq", "ex"), None),
        P(("sq", "ex")),
        P(),
        P(("sq", "ex"), None),
        P(),
        P(),
        P(None, None, "sq"),
        P("sq", None),
        P(),
        P(),
        P("ex", None, None, None),
        P("ex", None, None),
    )
    return jax.shard_map(
        body,
        mesh=mesh,
        in_specs=placed,
        out_specs=(P(("sq", "ex"), None), P(("sq", "ex"), None)),
        check_vma=False,
    )
```

time: 511 us -> 314 us (0.61)
  local copies, waits for them, and re-layouts: 140 us -> 36.8 us
  matrix products: 127 us -> 31.1 us
  other arithmetic: 46.3 us -> 7.53 us
  starting transfers between devices: 13.2 us -> 46.9 us
  Pallas kernels: 0 us -> 25.7 us
  waiting for transfers between devices: 113 us -> 94.7 us
    gather x4 -> x2, local copies, waits for them, and re-layouts: 101 us -> 1.15 us  [the longest x1 0.58 us: body(): jnp.take(ranks, plane_sources(ex_index, core), axis=0, mode='clip')]
    dot_general x34 -> x4, matrix products: 109 us -> 12.8 us  [the longest x1 5.1 us: body(): jnp.einsum('sekd,edf->sekf', grouped, expert_in[:, 1], preferred_element_...]
    all_gather x3 -> x0, waiting for transfers between devices: 47.7 us -> none  [the longest x1 41.4 us: body(): lax.all_gather(normed, 'sq', axis=0, tiled=True)]
    reduce_sum x20 -> x0, other arithmetic: 39.3 us -> none  [the longest x16 35.4 us: online_block(): row_total = row_total * factor + jnp.sum(probs, axis=1)]
    ppermute x0 -> x15, waiting for transfers between devices: none -> 33.5 us  [the longest x6 24.2 us: plane_shift(): return lax.ppermute(array, 'ex', pairs)]
    ppermute x0 -> x15, starting transfers between devices: none -> 29.1 us  [the longest x8 18.5 us: ring_shift(): lax.ppermute(array, 'sq', [(i, (i + amount) % count) for i in range(count)])]
    pallas_call x0 -> x2, Pallas kernels: none -> 25.7 us  [flash_part(): pl.pallas_call(functools.partial(flash_kernel, 1024, scale), out_shape=ja...]
    unnamed x22 -> x45, local copies, waits for them, and re-layouts: 6.29 us -> 19.4 us
  transfers between devices with their start and end apart: 6 -> 18, of which waited for: 4 -> 11; matrix products, arithmetic and copies ran while one was open for 46% -> 13% of each run, Pallas kernels for 0% -> 8%
where the time goes in v1:
time: 314 us; the launch traced here: 313 us
  waiting for transfers between devices  94.7 us (30%)
  blocking collectives  56.2 us (18%)
  starting transfers between devices  46.9 us (15%)
  local copies, waits for them, and re-layouts  36.8 us (12%)
  matrix products  31.1 us (10%)
  Pallas kernels  25.7 us (8%)
  between operations  14.4 us (5%)
  other arithmetic  7.53 us (2%)
    all_to_all x1, blocking collectives, body(): lax.all_to_all(outgoing, 'ex', split_axis=0, concat_axis=0, tiled=True)  56.2 us
    all_to_all x1, waiting for transfers between devices, body(): lax.all_to_all(produced.reshape(ex_count * local_experts, slot_count, mod...  52.1 us
    pallas_call x2, Pallas kernels, flash_part(): pl.pallas_call(functools.partial(flash_kernel, 1024, scale), out_shape=ja...  25.7 us
    ppermute x6, waiting for transfers between devices, plane_shift(): return lax.ppermute(array, 'ex', pairs)  24.2 us
    unnamed x45, local copies, waits for them, and re-layouts  19.4 us
    ppermute x8, starting transfers between devices, ring_shift(): lax.ppermute(array, 'sq', [(i, (i + amount) % count) for i in range(count)])  18.5 us
    dot_general x1, matrix products, body(): jnp.einsum('sekf,efd->sekd', hidden, expert_out, preferred_element_type=j...  12.4 us
    all_to_all x1, starting transfers between devices, body(): lax.all_to_all(head_out, 'sq', split_axis=0, concat_axis=1, tiled=True)  11.6 us
  transfers between devices with their start and end apart: 18, of which 11 were waited for; matrix products, arithmetic and copies ran while one was open for 13% of the time, Pallas kernels for 8%

profile of v1, /device:TPU:8, one launch (start us, length us, event | category | flops | bytes accessed | tf_op | source)
XLA Modules:
  0.0 313.2 jit_solution(8321054489045276767)
XLA Ops:
  11.1 3.3 %collective-permute-start = (bf16[64,2048]{1,0:T(8,128)(2,1)}, bf16[64,2048]{1,0:T(8,128)(2,1)}, u32[]{:S(2)}, u32[]{:S(2)}) collective-permute-start(bf16[64,2048]{1,0:T(8,128)(2,1)} %multiply_convert_fusion.1), channel_id=1, source_target_pairs={{0,64},{32,96},{64,128},{96,160},{128,192},{160,224},{192,0},{224,... | collective-permute-start | bytes 786440 | tf_op jit(solution)/shard_map/ppermute | solution.py:116
  14.4 3.0 collective-permute-start.4
  17.4 8.6 %collective-permute-done = bf16[64,2048]{1,0:T(8,128)(2,1)} collective-permute-done((bf16[64,2048]{1,0:T(8,128)(2,1)}, bf16[64,2048]{1,0:T(8,128)(2,1)}, u32[]{:S(2)}, u32[]{:S(2)}) %collective-permute-start) | collective-permute-done | bytes 262176 | tf_op jit(solution)/shard_map/ppermute | solution.py:116
  26.0 4.6 %collective-permute-start.1 = (bf16[64,2048]{1,0:T(8,128)(2,1)}, bf16[64,2048]{1,0:T(8,128)(2,1)}, u32[]{:S(2)}, u32[]{:S(2)}) collective-permute-start(bf16[64,2048]{1,0:T(8,128)(2,1)} %collective-permute-done), channel_id=1, source_target_pairs={{0,32},{32,64},{64,96},{96,128},{128,160},{160,192},{192,224},{224... | collective-permute-start | bytes 786440 | tf_op jit(solution)/shard_map/ppermute | solution.py:116
  30.8 3.1 collective-permute-start.3
  33.9 2.6 copy.32
  39.0 2.7 collective-permute-start.7
  41.7 1.7 constant_dynamic-update-slice_fusion.8
  43.4 1.7 constant_dynamic-update-slice_fusion.7
  47.0 1.9 constant_dynamic-update-slice_fusion.5
  48.9 1.7 constant_dynamic-update-slice_fusion.4
  53.7 3.3 %convolution_convert_fusion.3 = bf16[512,384]{1,0:T(8,128)(2,1)S(1)} fusion(bf16[512,2048]{1,0:T(8,128)(2,1)} %constant_dynamic-update-slice_fusion, bf16[2048,384]{0,1:T(8,128)(2,1)} %bitcast.113), kind=kOutput, calls=%fused_computation.22 | convolution fusion | flops 805502976 | bytes 4063232 | tf_op jit(solution)/shard_map/dot_general | solution.py:162
  59.3 3.0 collective-permute-start.10
  62.9 2.6 collective-permute-start.9
  67.2 2.8 collective-permute-done.8
  72.3 2.3 collective-permute-start.13
  76.7 8.3 %collective-permute-done.11 = bf16[2048,256]{1,0:T(8,128)(2,1)S(1)} collective-permute-done((bf16[2048,256]{1,0:T(8,128)(2,1)S(1)}, bf16[2048,256]{1,0:T(8,128)(2,1)S(1)}, u32[]{:S(2)}, u32[]{:S(2)}) %collective-permute-start.11) | collective-permute-done | bytes 1048608 | tf_op jit(solution)/shard_map/ppermute | solution.py:90
  87.6 10.9 %collective-permute-done.13 = bf16[2048,256]{1,0:T(8,128)(2,1)S(1)} collective-permute-done((bf16[2048,256]{1,0:T(8,128)(2,1)S(1)}, bf16[2048,256]{1,0:T(8,128)(2,1)S(1)}, u32[]{:S(2)}, u32[]{:S(2)}) %collective-permute-start.13) | collective-permute-done | bytes 1048608 | tf_op jit(solution)/shard_map/ppermute | solution.py:90
  102.6 5.1 %broadcast_in_dim.77.key_rank_ref = s32[8192,128]{1,0:T(8,128)} broadcast(s32[8192]{0:T(1024)S(1)} %bitcast.115), dimensions={0} | broadcast | bytes 4227072 | tf_op jit(solution)/shard_map/broadcast_in_dim | solution.py:62
  107.7 12.9 %flash_part.2.state_ref = f32[136,512]{1,0:T(8,128)S(1)} custom-call(bf16[512,128]{1,0:T(8,128)(2,1)S(1)} %slice.46.query_ref, bf16[8192,256]{1,0:T(8,128)(2,1)} %constant_dynamic-update-slice_fusion.9.keyval_ref, s32[1,512]{1,0:T(1,128)S(1)} %constant_dynamic-slice_fusion.query_rank_ref, s32[8192,128]{1,0:T(8,128)} %broadcast_in_dim.77.key_rank_ref, ...), custom_call_target="tpu_custom_call" | custom-call | tf_op jit(solution)/shard_map/flash_part/pallas_call | solution.py:63
  120.6 5.1 %broadcast_in_dim.74.key_rank_ref = s32[8192,128]{1,0:T(8,128)} broadcast(s32[8192]{0:T(1024)S(1)} %bitcast.116), dimensions={0} | broadcast | bytes 4227072 | tf_op jit(solution)/shard_map/broadcast_in_dim | solution.py:62
  125.7 12.9 %flash_part.3 = f32[136,512]{1,0:T(8,128)S(1)} custom-call(bf16[512,128]{1,0:T(8,128)(2,1)S(1)} %slice.46.query_ref, bf16[8192,256]{1,0:T(8,128)(2,1)} %collective-permute-done.14.keyval_ref, s32[1,512]{1,0:T(1,128)S(1)} %constant_dynamic-slice_fusion.query_rank_ref, s32[8192,128]{1,0:T(8,128)} %broadcast_in_dim.74.key_rank_ref, ...), custom_call_target="tpu_custom_call" | custom-call | tf_op jit(solution)/shard_map/flash_part/pallas_call | solution.py:63
  139.4 11.6 %all-to-all-start = ((bf16[8,64,128]{2,1,0:T(8,128)(2,1)}), bf16[8,64,128]{2,1,0:T(8,128)(2,1)S(1)}, u32[]{:S(2)}, u32[]{:S(2)}) async-start(bf16[8,64,128]{2,1,0:T(8,128)(2,1)} %bitcast.6), calls=%async_computation | async-start | bytes 262144 | tf_op jit(solution)/shard_map/all_to_all | solution.py:191
  151.7 9.1 %all-to-all-done = bf16[8,64,128]{2,1,0:T(8,128)(2,1)S(1)} async-done(((bf16[8,64,128]{2,1,0:T(8,128)(2,1)}), bf16[8,64,128]{2,1,0:T(8,128)(2,1)S(1)}, u32[]{:S(2)}, u32[]{:S(2)}) %all-to-all-start) | async-done | bytes 131104 | tf_op jit(solution)/shard_map/all_to_all | solution.py:191
  160.8 3.0 convert_reduce_fusion
  166.0 56.2 %all_to_all.26 = bf16[32,32,2048]{2,1,0:T(8,128)(2,1)S(1)} all-to-all(bf16[32,32,2048]{2,1,0:T(8,128)(2,1)S(1)} %bitcast.111), channel_id=1, replica_groups=mesh['sq'=8,'ex'=32] {'ex'}, dimensions={0} | all-to-all | bytes 8388608 | tf_op jit(solution)/shard_map/all_to_all | solution.py:219
  222.2 2.0 copy-done.5
  224.3 5.1 %fusion.1 = f32[32,32,768]{2,1,0:T(8,128)} fusion(bf16[32,32,2048]{2,1,0:T(8,128)(2,1)S(1)} %all_to_all.26, bf16[1,2,2048,768]{3,2,1,0:T(8,128)(2,1)S(1)} %bitcast.121), kind=kOutput, calls=%fused_computation.7 | convolution fusion | flops 3221225472 | bytes 10485760 | tf_op jit(solution)/shard_map/sekd,edf->sekf/dot_general | solution.py:225
  229.4 12.4 %convolution_convert_fusion = bf16[32,32,2048]{2,1,0:T(8,128)(2,1)} fusion(bf16[1,768,2048]{2,1,0:T(8,128)(2,1)S(1)} %copy-done, f32[32,32,768]{2,1,0:T(8,128)} %fusion.1, bf16[32,32,2048]{2,1,0:T(8,128)(2,1)} %copy-done.5, bf16[1,2,2048,768]{3,2,1,0:T(8,128)(2,1)} %param.26), kind=kOutput, calls=%fused_computation.3 | convolution fusion | flops 6449266688 | bytes 17825792 | tf_op jit(solution)/shard_map/sekf,efd->sekd/dot_general | solution.py:229
  241.7 6.1 %all-to-all-start.2 = ((bf16[32,32,2048]{2,1,0:T(8,128)(2,1)}), bf16[32,32,2048]{2,1,0:T(8,128)(2,1)}, u32[]{:S(2)}, u32[]{:S(2)}) async-start(bf16[32,32,2048]{2,1,0:T(8,128)(2,1)} %convolution_convert_fusion), calls=%async_computation.2 | async-start | bytes 8388608 | tf_op jit(solution)/shard_map/all_to_all | solution.py:232
  250.4 52.1 %all-to-all-done.2 = bf16[32,32,2048]{2,1,0:T(8,128)(2,1)} async-done(((bf16[32,32,2048]{2,1,0:T(8,128)(2,1)}), bf16[32,32,2048]{2,1,0:T(8,128)(2,1)}, u32[]{:S(2)}, u32[]{:S(2)}) %all-to-all-start.2) | async-done | bytes 4194336 | tf_op jit(solution)/shard_map/all_to_all | solution.py:232
  302.5 3.1 %fusion.29 = f32[128,2048]{1,0:T(8,128)S(1)} fusion(bf16[1024,2048]{1,0:T(8,128)(2,1)} %bitcast.30, bf16[64,1024]{0,1:T(8,128)(2,1)} %fusion.26, bf16[64,1024]{0,1:T(8,128)(2,1)S(1)} %fusion.25), kind=kOutput, calls=%fused_computation.47 | convolution fusion | flops 537395200 | bytes 5505024 | tf_op jit(solution)/shard_map/dot_general | solution.py:246
  (114 shorter events, 34.1 us)
Async XLA Ops:
  7.2 222.2 %copy-start = (bf16[1,768,2048]{2,1,0:T(8,128)(2,1)S(1)}, bf16[1,768,2048]{2,1,0:T(8,128)(2,1)}, u32[]{:S(2)}) copy-start(bf16[1,768,2048]{2,1,0:T(8,128)(2,1)} %param.27) | copy-start | bytes 9437188
  7.2 153.6 %all-gather.2.cloned.1.call-start = ((), (), s32[]{:S(2)}) async-start(), calls=%async_computation.3 | async-start | bytes 4718592 | tf_op jit(solution)/shard_map/all_gather | solution.py:192
  8.8 0.8 copy-start.3
  8.8 38.3 %copy-start.9 = (f32[2048]{0:T(1024)S(1)}, f32[2048]{0:T(1024)}, u32[]{:S(2)}) copy-start(f32[2048]{0:T(1024)} %param.21) | copy-start | bytes 24580
  11.1 14.9 %collective-permute-start = (bf16[64,2048]{1,0:T(8,128)(2,1)}, bf16[64,2048]{1,0:T(8,128)(2,1)}, u32[]{:S(2)}, u32[]{:S(2)}) collective-permute-start(bf16[64,2048]{1,0:T(8,128)(2,1)} %multiply_convert_fusion.1), channel_id=1, source_target_pairs={{0,64},{32,96},{64,128},{96,160},{128,192},{160,224},{192,0},{224,... | collective-permute-start | bytes 786440 | tf_op jit(solution)/shard_map/ppermute | solution.py:116
  14.4 24.7 %collective-permute-start.4 = (bf16[64,2048]{1,0:T(8,128)(2,1)}, bf16[64,2048]{1,0:T(8,128)(2,1)S(1)}, u32[]{:S(2)}, u32[]{:S(2)}) collective-permute-start(bf16[64,2048]{1,0:T(8,128)(2,1)} %multiply_convert_fusion.1), channel_id=1, source_target_pairs={{0,192},{32,224},{64,0},{96,32},{128,64},{160,96},{192,128},{224,1... | collective-permute-start | bytes 786440 | tf_op jit(solution)/shard_map/ppermute | solution.py:116
  26.0 15.7 %collective-permute-start.1 = (bf16[64,2048]{1,0:T(8,128)(2,1)}, bf16[64,2048]{1,0:T(8,128)(2,1)}, u32[]{:S(2)}, u32[]{:S(2)}) collective-permute-start(bf16[64,2048]{1,0:T(8,128)(2,1)} %collective-permute-done), channel_id=1, source_target_pairs={{0,32},{32,64},{64,96},{96,128},{128,160},{160,192},{192,224},{224... | collective-permute-start | bytes 786440 | tf_op jit(solution)/shard_map/ppermute | solution.py:116
  30.6 14.7 %collective-permute-start.2 = (bf16[64,2048]{1,0:T(8,128)(2,1)}, bf16[64,2048]{1,0:T(8,128)(2,1)}, u32[]{:S(2)}, u32[]{:S(2)}) collective-permute-start(bf16[64,2048]{1,0:T(8,128)(2,1)} %multiply_convert_fusion.1), channel_id=1, source_target_pairs={{0,32},{32,64},{64,96},{96,128},{128,160},{160,192},{192,224},{224... | collective-permute-start | bytes 786440 | tf_op jit(solution)/shard_map/ppermute | solution.py:116
  30.8 18.1 %collective-permute-start.3 = (bf16[64,2048]{1,0:T(8,128)(2,1)}, bf16[64,2048]{1,0:T(8,128)(2,1)}, u32[]{:S(2)}, u32[]{:S(2)}) collective-permute-start(bf16[64,2048]{1,0:T(8,128)(2,1)} %multiply_convert_fusion.1), channel_id=1, source_target_pairs={{0,224},{32,0},{64,32},{96,64},{128,96},{160,128},{192,160},{224,1... | collective-permute-start | bytes 786440 | tf_op jit(solution)/shard_map/ppermute | solution.py:116
  37.4 14.9 %collective-permute-start.6 = (bf16[32,2048]{1,0:T(8,128)(2,1)S(1)}, bf16[32,2048]{1,0:T(8,128)(2,1)S(1)}, u32[]{:S(2)}, u32[]{:S(2)}) collective-permute-start(bf16[32,2048]{1,0:T(8,128)(2,1)S(1)} %slice.44), channel_id=1, source_target_pairs={{0,64},{32,96},{64,128},{96,160},{128,192},{160,224},{192,0},{224,... | collective-permute-start | bytes 393224 | tf_op jit(solution)/shard_map/ppermute | solution.py:116
  39.0 14.0 %collective-permute-start.7 = (bf16[32,2048]{1,0:T(8,128)(2,1)S(1)}, bf16[32,2048]{1,0:T(8,128)(2,1)S(1)}, u32[]{:S(2)}, u32[]{:S(2)}) collective-permute-start(bf16[32,2048]{1,0:T(8,128)(2,1)S(1)} %slice.45), channel_id=1, source_target_pairs={{0,192},{32,224},{64,0},{96,32},{128,64},{160,96},{192,128},{224,1... | collective-permute-start | bytes 393224 | tf_op jit(solution)/shard_map/ppermute | solution.py:116
  41.7 9.9 %collective-permute-start.5 = (bf16[64,2048]{1,0:T(8,128)(2,1)S(1)}, bf16[64,2048]{1,0:T(8,128)(2,1)S(1)}, u32[]{:S(2)}, u32[]{:S(2)}) collective-permute-start(bf16[64,2048]{1,0:T(8,128)(2,1)S(1)} %collective-permute-done.4), channel_id=1, source_target_pairs={{0,224},{32,0},{64,32},{96,64},{128,96},{160,128},{192,160},{224,1... | collective-permute-start | bytes 786440 | tf_op jit(solution)/shard_map/ppermute | solution.py:116
  59.3 7.9 %collective-permute-start.10 = (bf16[512,256]{1,0:T(8,128)(2,1)S(1)}, bf16[512,256]{1,0:T(8,128)(2,1)S(1)}, u32[]{:S(2)}, u32[]{:S(2)}) collective-permute-start(bf16[512,256]{1,0:T(8,128)(2,1)S(1)} %get-tuple-element.9), channel_id=1, source_target_pairs={{0,16},{1,5},{2,18},{3,7},{4,20},{5,1},{6,22},{7,3},{8,24},{9,13},... | collective-permute-start | bytes 786440 | tf_op jit(solution)/shard_map/ppermute | solution.py:90
  62.3 7.7 %collective-permute-start.8 = (bf16[512,256]{1,0:T(8,128)(2,1)S(1)}, bf16[512,256]{1,0:T(8,128)(2,1)S(1)}, u32[]{:S(2)}, u32[]{:S(2)}) collective-permute-start(bf16[512,256]{1,0:T(8,128)(2,1)S(1)} %get-tuple-element.9), channel_id=1, source_target_pairs={{0,8},{1,3},{2,10},{3,5},{4,12},{5,7},{6,14},{7,1},{8,16},{9,11},{... | collective-permute-start | bytes 786440 | tf_op jit(solution)/shard_map/ppermute | solution.py:90
  62.9 7.2 %collective-permute-start.9 = (bf16[512,256]{1,0:T(8,128)(2,1)S(1)}, bf16[512,256]{1,0:T(8,128)(2,1)S(1)}, u32[]{:S(2)}, u32[]{:S(2)}) collective-permute-start(bf16[512,256]{1,0:T(8,128)(2,1)S(1)} %get-tuple-element.9), channel_id=1, source_target_pairs={{0,24},{1,7},{2,26},{3,1},{4,28},{5,3},{6,30},{7,5},{8,0},{9,15},{... | collective-permute-start | bytes 786440 | tf_op jit(solution)/shard_map/ppermute | solution.py:90
  70.2 14.9 %collective-permute-start.11 = (bf16[2048,256]{1,0:T(8,128)(2,1)S(1)}, bf16[2048,256]{1,0:T(8,128)(2,1)S(1)}, u32[]{:S(2)}, u32[]{:S(2)}) collective-permute-start(bf16[2048,256]{1,0:T(8,128)(2,1)S(1)} %pad_maximum_fusion), channel_id=1, source_target_pairs={{0,2},{1,9},{2,4},{3,11},{4,6},{5,13},{6,0},{7,15},{8,10},{9,17},{... | collective-permute-start | bytes 3145736 | tf_op jit(solution)/shard_map/ppermute | solution.py:90
  71.8 14.8 %collective-permute-start.12 = (bf16[2048,256]{1,0:T(8,128)(2,1)S(1)}, bf16[2048,256]{1,0:T(8,128)(2,1)S(1)}, u32[]{:S(2)}, u32[]{:S(2)}) collective-permute-start(bf16[2048,256]{1,0:T(8,128)(2,1)S(1)} %pad_maximum_fusion), channel_id=1, source_target_pairs={{0,6},{1,25},{2,0},{3,27},{4,2},{5,29},{6,4},{7,31},{8,14},{9,1},{... | collective-permute-start | bytes 3145736 | tf_op jit(solution)/shard_map/ppermute | solution.py:90
  72.3 26.3 %collective-permute-start.13 = (bf16[2048,256]{1,0:T(8,128)(2,1)S(1)}, bf16[2048,256]{1,0:T(8,128)(2,1)S(1)}, u32[]{:S(2)}, u32[]{:S(2)}) collective-permute-start(bf16[2048,256]{1,0:T(8,128)(2,1)S(1)} %pad_maximum_fusion), channel_id=1, source_target_pairs={{0,4},{1,17},{2,6},{3,19},{4,0},{5,21},{6,2},{7,23},{8,12},{9,25},... | collective-permute-start | bytes 3145736 | tf_op jit(solution)/shard_map/ppermute | solution.py:90
  76.7 22.9 %copy-start.12 = (s32[4]{0:T(128)S(1)}, s32[4]{0:T(128)}, u32[]{:S(2)}) copy-start(s32[4]{0:T(128)} %constant.130.clone) | copy-start | bytes 52
  76.7 23.3 %copy-start.8 = (s32[16384]{0:T(1024)S(1)}, s32[16384]{0:T(1024)}, u32[]{:S(2)}) copy-start(s32[16384]{0:T(1024)} %param.18) | copy-start | bytes 196612
  99.6 21.0 %collective-permute-start.14 = (bf16[8192,256]{1,0:T(8,128)(2,1)}, bf16[8192,256]{1,0:T(8,128)(2,1)}, u32[]{:S(2)}, u32[]{:S(2)}) collective-permute-start(bf16[8192,256]{1,0:T(8,128)(2,1)} %constant_dynamic-update-slice_fusion.9.keyval_ref), channel_id=1, source_target_pairs={{0,1},{1,0},{2,3},{3,2},{4,5},{5,4},{6,7},{7,6},{8,9},{9,8},{10,11... | collective-permute-start | bytes 12582920 | tf_op jit(solution)/shard_map/ppermute | solution.py:111
  125.7 25.3 %copy-start.11 = (s32[64,6]{0,1:T(8,128)S(1)}, s32[64,6]{0,1:T(8,128)}, u32[]{:S(2)}) copy-start(s32[64,6]{0,1:T(8,128)} %param.19) | copy-start | bytes 4612
  139.4 21.4 %all-to-all-start = ((bf16[8,64,128]{2,1,0:T(8,128)(2,1)}), bf16[8,64,128]{2,1,0:T(8,128)(2,1)S(1)}, u32[]{:S(2)}, u32[]{:S(2)}) async-start(bf16[8,64,128]{2,1,0:T(8,128)(2,1)} %bitcast.6), calls=%async_computation | async-start | bytes 262144 | tf_op jit(solution)/shard_map/all_to_all | solution.py:191
  160.8 3.0 copy-start.4
  160.8 3.9 %copy-start.10 = (f32[2048]{0:T(1024)S(1)}, f32[2048]{0:T(1024)}, u32[]{:S(2)}) copy-start(f32[2048]{0:T(1024)} %param.24) | copy-start | bytes 24580
  164.6 1.3 copy-start.1
  164.7 59.6 %slice-start = ((s8[6291456]{0:T(1024)(128)(4,1)}), s8[4194304]{0:T(1024)(128)(4,1)S(1)}, s32[]{:S(2)}) async-start(s8[6291456]{0:T(1024)(128)(4,1)} %bitcast.120), calls=%async_computation.4 | async-start | bytes 8388608
  166.0 58.2 %slice-start.1 = ((s8[6291456]{0:T(1024)(128)(4,1)}), s8[2097152]{0:T(1024)(128)(4,1)S(1)}, s32[]{:S(2)}) async-start(s8[6291456]{0:T(1024)(128)(4,1)} %bitcast.120), calls=%async_computation.5 | async-start | bytes 4194304
  222.2 2.0 copy-start.5
  241.7 6.2 %copy-start.7 = (bf16[2048,32]{0,1:T(8,128)(2,1)S(1)}, bf16[2048,32]{0,1:T(8,128)(2,1)}, u32[]{:S(2)}) copy-start(bf16[2048,32]{0,1:T(8,128)(2,1)} %param.25) | copy-start | bytes 393220
  241.7 60.7 %all-to-all-start.2 = ((bf16[32,32,2048]{2,1,0:T(8,128)(2,1)}), bf16[32,32,2048]{2,1,0:T(8,128)(2,1)}, u32[]{:S(2)}, u32[]{:S(2)}) async-start(bf16[32,32,2048]{2,1,0:T(8,128)(2,1)} %convolution_convert_fusion), calls=%async_computation.2 | async-start | bytes 8388608 | tf_op jit(solution)/shard_map/all_to_all | solution.py:232
  302.5 3.1 %copy-start.2 = (f32[64,2048]{1,0:T(8,128)S(1)}, f32[64,2048]{1,0:T(8,128)}, u32[]{:S(2)}) copy-start(f32[64,2048]{1,0:T(8,128)} %copy-done.1) | copy-start | bytes 1572868
  (1 other events, 0.8 us)
Sparse Core Ops, SparseCore 0:
  53.8 58.1 all-gather.1

commit v2 on v1

--- a/solution.py
+++ b/solution.py
@@ -56,16 +56,19 @@
     )
 
 
+def spread_rank(key_rank):
+    return jnp.broadcast_to(key_rank[:, None], (key_rank.shape[0], 128))
+
+
 def flash_part(queries, keyval, query_rank, key_rank, state):
     head_dim = queries.shape[1]
     scale = math.log2(math.e) / math.sqrt(head_dim)
-    wide_rank = jnp.broadcast_to(key_rank[:, None], (key_rank.shape[0], 128))
     return pl.pallas_call(
         functools.partial(flash_kernel, 1024, scale),
         out_shape=jax.ShapeDtypeStruct(state.shape, jnp.float32),
         name="flash_part",
         compiler_params=pltpu.CompilerParams(vmem_limit_bytes=48 << 20),
-    )(queries, keyval, query_rank[None, :], wide_rank, state)
+    )(queries, keyval, query_rank[None, :], key_rank, state)
 
 
 side = 4
@@ -126,7 +129,7 @@
     m3 = ring_shift(m2, -1)
     p4 = ring_shift(p2[:half], 2)
     m4 = ring_shift(m2[half:], -2)
-    return jnp.concatenate([p3, p2, p1, array, m1, m2, m3, p4, m4], axis=0)
+    return [p3, p2, p1, array, m1, m2, m3, jnp.concatenate([p4, m4], axis=0)]
 
 
 def body(
@@ -157,24 +160,28 @@
     normed = rms_norm(base_rows, attn_gain).astype(jnp.bfloat16)
     flat_qkv = w_qkv.reshape(model_width, 3 * head_dim)
     sq_index = lax.axis_index("sq")
-    stream = ring_gather(normed)
-    stream, w_out = lax.optimization_barrier((stream, w_out))
-    rolled = jnp.dot(stream, flat_qkv, preferred_element_type=jnp.float32).astype(jnp.bfloat16)
-    group_rows = rolled.shape[0]
-    projected = lax.dynamic_slice_in_dim(
-        jnp.concatenate([rolled, rolled], axis=0),
-        (3 - sq_index) % sq_count * tok_rows,
-        group_rows,
-        axis=0,
-    )
-    queries = projected[:, :head_dim]
-    keyval = projected[:, head_dim:]
+    group_rows = sq_count * tok_rows
     ranks = time_rank.reshape(sq_count, ex_count, tok_rows).transpose(1, 0, 2)
     ranks = ranks.reshape(ex_count, group_rows)
     core = ex_index % cores
     query_rank = lax.dynamic_index_in_dim(ranks, ex_index, 0, keepdims=False)
     near_rank = jnp.take(ranks, plane_sources(ex_index, core), axis=0, mode="clip").reshape(-1)
     far_rank = jnp.take(ranks, plane_sources(ex_index, 1 - core), axis=0, mode="clip").reshape(-1)
+    near_rank, far_rank = spread_rank(near_rank), spread_rank(far_rank)
+    pieces = ring_gather(normed)
+    late = lax.optimization_barrier((pieces[0], pieces[6], pieces[7], near_rank, far_rank))
+    pieces = [late[0]] + pieces[1:6] + [late[1], late[2]]
+    near_rank, far_rank = late[3:]
+    projected = jnp.zeros((group_rows, 3 * head_dim), jnp.bfloat16)
+    for b in (3, 2, 4, 1, 5, 0, 6, 7):
+        piece = jnp.dot(pieces[b], flat_qkv, preferred_element_type=jnp.float32)
+        place = (sq_index + (b + 5)) % sq_count * tok_rows
+        projected = lax.dynamic_update_slice_in_dim(
+            projected, piece.astype(jnp.bfloat16), place, axis=0
+        )
+    projected, w_out = lax.optimization_barrier((projected, w_out))
+    queries = projected[:, :head_dim]
+    keyval = projected[:, head_dim:]
     near = plane_gather(keyval)
     far = core_swap(near)
     state = jnp.concatenate(

time: 314 us -> 306 us (0.975)
  matrix products: 31.1 us -> 43.2 us
  waiting for transfers between devices: 94.7 us -> 85.4 us
  starting transfers between devices: 46.9 us -> 40.2 us
    dot_general x1 -> x8, matrix products: 3.31 us -> 15.5 us  [body(): piece = jnp.dot(pieces[b], flat_qkv, preferred_element_type=jnp.float32)]
    ppermute x8, waiting for transfers between devices: 9.24 us -> 0.02 us  [ring_shift(): lax.ppermute(array, 'sq', [(i, (i + amount) % count) for i in range(count)])]
    unnamed x45 -> x32, local copies, waits for them, and re-layouts: 19.4 us -> 10.5 us
    all_to_all x1, starting transfers between devices: 11.6 us -> 6.22 us  [body(): lax.all_to_all(head_out, 'sq', split_axis=0, concat_axis=1, tiled=True)]
    broadcast_in_dim x2 -> x3, local copies, waits for them, and re-layouts: 10.2 us -> 10.9 us  [the longest x2 10.1 us: spread_rank(): return jnp.broadcast_to(key_rank[:, None], (key_rank.shape[0], 128))]
  transfers between devices with their start and end apart: 18 -> 18, of which waited for: 11 -> 8; matrix products, arithmetic and copies ran while one was open for 13% -> 12% of each run, Pallas kernels for 8% -> 8%
where the time goes in v2:
time: 306 us; the launch traced here: 305 us
  waiting for transfers between devices  85.4 us (28%)
  blocking collectives  56.8 us (19%)
  matrix products  43.2 us (14%)
  starting transfers between devices  40.2 us (13%)
  local copies, waits for them, and re-layouts  34.4 us (11%)
  Pallas kernels  25.8 us (8%)
  between operations  14.4 us (5%)
  other arithmetic  4.98 us (2%)
    all_to_all x1, blocking collectives, body(): lax.all_to_all(outgoing, 'ex', split_axis=0, concat_axis=0, tiled=True)  56.8 us
    all_to_all x1, waiting for transfers between devices, body(): lax.all_to_all(produced.reshape(ex_count * local_experts, slot_count, mod...  52 us
    pallas_call x2, Pallas kernels, flash_part(): pl.pallas_call(functools.partial(flash_kernel, 1024, scale), out_shape=ja...  25.8 us
    ppermute x6, waiting for transfers between devices, plane_shift(): return lax.ppermute(array, 'ex', pairs)  24.2 us
    ppermute x8, starting transfers between devices, ring_shift(): lax.ppermute(array, 'sq', [(i, (i + amount) % count) for i in range(count)])  17.2 us
    dot_general x8, matrix products, body(): piece = jnp.dot(pieces[b], flat_qkv, preferred_element_type=jnp.float32)  15.5 us
    dot_general x1, matrix products, body(): jnp.einsum('sekf,efd->sekd', hidden, expert_out, preferred_element_type=j...  12.3 us
    ppermute x6, starting transfers between devices, plane_shift(): return lax.ppermute(array, 'ex', pairs)  10.7 us
  transfers between devices with their start and end apart: 18, of which 8 were waited for; matrix products, arithmetic and copies ran while one was open for 12% of the time, Pallas kernels for 8%

profile of v2, /device:TPU:8, one launch (start us, length us, event | category | flops | bytes accessed | tf_op | source)
XLA Modules:
  0.0 305.2 jit_solution(10612519136223567034)
XLA Ops:
  10.4 3.3 %collective-permute-start.2 = (bf16[64,2048]{1,0:T(8,128)(2,1)S(1)}, bf16[64,2048]{1,0:T(8,128)(2,1)}, u32[]{:S(2)}, u32[]{:S(2)}) collective-permute-start(bf16[64,2048]{1,0:T(8,128)(2,1)S(1)} %multiply_convert_fusion.1), channel_id=1, source_target_pairs={{0,64},{32,96},{64,128},{96,160},{128,192},{160,224},{192,0},{224,... | collective-permute-start | bytes 786440 | tf_op jit(solution)/shard_map/ppermute | solution.py:119
  13.7 3.1 %collective-permute-start.3 = (bf16[64,2048]{1,0:T(8,128)(2,1)S(1)}, bf16[64,2048]{1,0:T(8,128)(2,1)}, u32[]{:S(2)}, u32[]{:S(2)}) collective-permute-start(bf16[64,2048]{1,0:T(8,128)(2,1)S(1)} %multiply_convert_fusion.1), channel_id=1, source_target_pairs={{0,192},{32,224},{64,0},{96,32},{128,64},{160,96},{192,128},{224,1... | collective-permute-start | bytes 786440 | tf_op jit(solution)/shard_map/ppermute | solution.py:119
  17.9 2.2 collective-permute-start.1
  28.0 2.6 copy.32
  31.5 2.6 fusion.21
  36.1 4.1 %collective-permute-start.7 = (bf16[32,2048]{1,0:T(8,128)(2,1)S(1)}, bf16[32,2048]{1,0:T(8,128)(2,1)S(1)}, u32[]{:S(2)}, u32[]{:S(2)}) collective-permute-start(bf16[32,2048]{1,0:T(8,128)(2,1)S(1)} %slice.45), channel_id=1, source_target_pairs={{0,192},{32,224},{64,0},{96,32},{128,64},{160,96},{192,128},{224,1... | collective-permute-start | bytes 393224 | tf_op jit(solution)/shard_map/ppermute | solution.py:119
  40.2 3.2 %collective-permute-start.5 = (bf16[64,2048]{1,0:T(8,128)(2,1)}, bf16[64,2048]{1,0:T(8,128)(2,1)S(1)}, u32[]{:S(2)}, u32[]{:S(2)}) collective-permute-start(bf16[64,2048]{1,0:T(8,128)(2,1)} %collective-permute-done.3), channel_id=1, source_target_pairs={{0,224},{32,0},{64,32},{96,64},{128,96},{160,128},{192,160},{224,1... | collective-permute-start | bytes 786440 | tf_op jit(solution)/shard_map/ppermute | solution.py:119
  43.4 2.7 fusion.20
  46.2 2.2 fusion.19
  48.3 2.2 fusion.18
  50.5 2.2 fusion.17
  52.7 5.1 %broadcast_in_dim.78.key_rank_ref = s32[8192,128]{1,0:T(8,128)} broadcast(s32[8192]{0:T(1024)S(1)} %bitcast.136), dimensions={0} | broadcast | bytes 4227072 | tf_op jit(solution)/shard_map/broadcast_in_dim | solution.py:60
  57.8 5.0 %broadcast_in_dim.81.key_rank_ref = s32[8192,128]{1,0:T(8,128)} broadcast(s32[8192]{0:T(1024)S(1)} %bitcast.137), dimensions={0} | broadcast | bytes 4227072 | tf_op jit(solution)/shard_map/broadcast_in_dim | solution.py:60
  66.5 1.7 fusion.57
  68.2 3.0 collective-permute-start.10
  71.8 2.6 collective-permute-start.9
  76.1 2.8 collective-permute-done.8
  81.1 2.3 collective-permute-start.13
  85.6 8.3 %collective-permute-done.11 = bf16[2048,256]{1,0:T(8,128)(2,1)S(1)} collective-permute-done((bf16[2048,256]{1,0:T(8,128)(2,1)S(1)}, bf16[2048,256]{1,0:T(8,128)(2,1)S(1)}, u32[]{:S(2)}, u32[]{:S(2)}) %collective-permute-start.11) | collective-permute-done | bytes 1048608 | tf_op jit(solution)/shard_map/ppermute | solution.py:93
  96.6 10.9 %collective-permute-done.13 = bf16[2048,256]{1,0:T(8,128)(2,1)S(1)} collective-permute-done((bf16[2048,256]{1,0:T(8,128)(2,1)S(1)}, bf16[2048,256]{1,0:T(8,128)(2,1)S(1)}, u32[]{:S(2)}, u32[]{:S(2)}) %collective-permute-start.13) | collective-permute-done | bytes 1048608 | tf_op jit(solution)/shard_map/ppermute | solution.py:93
  109.6 12.9 %flash_part.2.state_ref = f32[136,512]{1,0:T(8,128)S(1)} custom-call(bf16[512,128]{1,0:T(8,128)(2,1)S(1)} %slice.32.query_ref, bf16[8192,256]{1,0:T(8,128)(2,1)} %constant_dynamic-update-slice_fusion.keyval_ref, s32[1,512]{1,0:T(1,128)S(1)} %constant_dynamic-slice_fusion.query_rank_ref, s32[8192,128]{1,0:T(8,128)} %broadcast_in_dim.78.key_rank_ref, ...), custom_call_target="tpu_custom_call" | custom-call | tf_op jit(solution)/shard_map/flash_part/pallas_call | solution.py:66
  122.5 12.9 %flash_part.3 = f32[136,512]{1,0:T(8,128)S(1)} custom-call(bf16[512,128]{1,0:T(8,128)(2,1)S(1)} %slice.32.query_ref, bf16[8192,256]{1,0:T(8,128)(2,1)} %collective-permute-done.14.keyval_ref, s32[1,512]{1,0:T(1,128)S(1)} %constant_dynamic-slice_fusion.query_rank_ref, s32[8192,128]{1,0:T(8,128)} %broadcast_in_dim.81.key_rank_ref, ...), custom_call_target="tpu_custom_call" | custom-call | tf_op jit(solution)/shard_map/flash_part/pallas_call | solution.py:66
  136.2 6.2 %all-to-all-start = ((bf16[8,64,128]{2,1,0:T(8,128)(2,1)}), bf16[8,64,128]{2,1,0:T(8,128)(2,1)S(1)}, u32[]{:S(2)}, u32[]{:S(2)}) async-start(bf16[8,64,128]{2,1,0:T(8,128)(2,1)} %bitcast.6), calls=%async_computation | async-start | bytes 262144 | tf_op jit(solution)/shard_map/all_to_all | solution.py:198
  143.1 9.1 %all-to-all-done = bf16[8,64,128]{2,1,0:T(8,128)(2,1)S(1)} async-done(((bf16[8,64,128]{2,1,0:T(8,128)(2,1)}), bf16[8,64,128]{2,1,0:T(8,128)(2,1)S(1)}, u32[]{:S(2)}, u32[]{:S(2)}) %all-to-all-start) | async-done | bytes 131104 | tf_op jit(solution)/shard_map/all_to_all | solution.py:198
  152.2 3.0 convert_reduce_fusion
  157.4 56.8 %all_to_all.26 = bf16[32,32,2048]{2,1,0:T(8,128)(2,1)S(1)} all-to-all(bf16[32,32,2048]{2,1,0:T(8,128)(2,1)S(1)} %bitcast.133), channel_id=1, replica_groups=mesh['sq'=8,'ex'=32] {'ex'}, dimensions={0} | all-to-all | bytes 8388608 | tf_op jit(solution)/shard_map/all_to_all | solution.py:226
  214.2 2.0 copy-done.6
  216.2 5.1 %fusion.1 = f32[32,32,768]{2,1,0:T(8,128)} fusion(bf16[32,32,2048]{2,1,0:T(8,128)(2,1)S(1)} %all_to_all.26, bf16[1,2,2048,768]{3,2,1,0:T(8,128)(2,1)S(1)} %bitcast.142), kind=kOutput, calls=%fused_computation.7 | convolution fusion | flops 3221225472 | bytes 10485760 | tf_op jit(solution)/shard_map/sekd,edf->sekf/dot_general | solution.py:232
  221.4 12.3 %convolution_convert_fusion = bf16[32,32,2048]{2,1,0:T(8,128)(2,1)} fusion(bf16[1,768,2048]{2,1,0:T(8,128)(2,1)S(1)} %copy-done, f32[32,32,768]{2,1,0:T(8,128)} %fusion.1, bf16[32,32,2048]{2,1,0:T(8,128)(2,1)} %copy-done.6, bf16[1,2,2048,768]{3,2,1,0:T(8,128)(2,1)} %param.26), kind=kOutput, calls=%fused_computation.3 | convolution fusion | flops 6449266688 | bytes 17825792 | tf_op jit(solution)/shard_map/sekf,efd->sekd/dot_general | solution.py:236
  233.7 6.1 %all-to-all-start.2 = ((bf16[32,32,2048]{2,1,0:T(8,128)(2,1)}), bf16[32,32,2048]{2,1,0:T(8,128)(2,1)}, u32[]{:S(2)}, u32[]{:S(2)}) async-start(bf16[32,32,2048]{2,1,0:T(8,128)(2,1)} %convolution_convert_fusion), calls=%async_computation.2 | async-start | bytes 8388608 | tf_op jit(solution)/shard_map/all_to_all | solution.py:239
  242.3 52.0 %all-to-all-done.2 = bf16[32,32,2048]{2,1,0:T(8,128)(2,1)} async-done(((bf16[32,32,2048]{2,1,0:T(8,128)(2,1)}), bf16[32,32,2048]{2,1,0:T(8,128)(2,1)}, u32[]{:S(2)}, u32[]{:S(2)}) %all-to-all-start.2) | async-done | bytes 4194336 | tf_op jit(solution)/shard_map/all_to_all | solution.py:239
  294.4 3.1 %fusion.36 = f32[128,2048]{1,0:T(8,128)S(1)} fusion(bf16[1024,2048]{1,0:T(8,128)(2,1)} %bitcast.30, bf16[64,1024]{0,1:T(8,128)(2,1)} %fusion.34, bf16[64,1024]{0,1:T(8,128)(2,1)S(1)} %fusion.33), kind=kOutput, calls=%fused_computation.60 | convolution fusion | flops 537395200 | bytes 5505024 | tf_op jit(solution)/shard_map/dot_general | solution.py:253
  (107 shorter events, 37.0 us)
Async XLA Ops:
  7.2 214.2 %copy-start = (bf16[1,768,2048]{2,1,0:T(8,128)(2,1)S(1)}, bf16[1,768,2048]{2,1,0:T(8,128)(2,1)}, u32[]{:S(2)}) copy-start(bf16[1,768,2048]{2,1,0:T(8,128)(2,1)} %param.27) | copy-start | bytes 9437188
  7.2 145.0 %all-gather.2.cloned.1.call-start = ((), (), s32[]{:S(2)}) async-start(), calls=%async_computation.3 | async-start | bytes 4718592 | tf_op jit(solution)/shard_map/all_gather | solution.py:199
  8.8 0.8 copy-start.4
  10.4 23.7 %collective-permute-start.2 = (bf16[64,2048]{1,0:T(8,128)(2,1)S(1)}, bf16[64,2048]{1,0:T(8,128)(2,1)}, u32[]{:S(2)}, u32[]{:S(2)}) collective-permute-start(bf16[64,2048]{1,0:T(8,128)(2,1)S(1)} %multiply_convert_fusion.1), channel_id=1, source_target_pairs={{0,64},{32,96},{64,128},{96,160},{128,192},{160,224},{192,0},{224,... | collective-permute-start | bytes 786440 | tf_op jit(solution)/shard_map/ppermute | solution.py:119
  13.7 21.5 %collective-permute-start.3 = (bf16[64,2048]{1,0:T(8,128)(2,1)S(1)}, bf16[64,2048]{1,0:T(8,128)(2,1)}, u32[]{:S(2)}, u32[]{:S(2)}) collective-permute-start(bf16[64,2048]{1,0:T(8,128)(2,1)S(1)} %multiply_convert_fusion.1), channel_id=1, source_target_pairs={{0,192},{32,224},{64,0},{96,32},{128,64},{160,96},{192,128},{224,1... | collective-permute-start | bytes 786440 | tf_op jit(solution)/shard_map/ppermute | solution.py:119
  16.8 23.4 %collective-permute-start = (bf16[64,2048]{1,0:T(8,128)(2,1)S(1)}, bf16[64,2048]{1,0:T(8,128)(2,1)}, u32[]{:S(2)}, u32[]{:S(2)}) collective-permute-start(bf16[64,2048]{1,0:T(8,128)(2,1)S(1)} %multiply_convert_fusion.1), channel_id=1, source_target_pairs={{0,32},{32,64},{64,96},{96,128},{128,160},{160,192},{192,224},{224... | collective-permute-start | bytes 786440 | tf_op jit(solution)/shard_map/ppermute | solution.py:119
  17.9 28.3 %collective-permute-start.1 = (bf16[64,2048]{1,0:T(8,128)(2,1)S(1)}, bf16[64,2048]{1,0:T(8,128)(2,1)}, u32[]{:S(2)}, u32[]{:S(2)}) collective-permute-start(bf16[64,2048]{1,0:T(8,128)(2,1)S(1)} %multiply_convert_fusion.1), channel_id=1, source_target_pairs={{0,224},{32,0},{64,32},{96,64},{128,96},{160,128},{192,160},{224,1... | collective-permute-start | bytes 786440 | tf_op jit(solution)/shard_map/ppermute | solution.py:119
  30.7 15.5 %copy-start.1 = (bf16[2048,3,128]{0,2,1:T(8,128)(2,1)S(1)}, bf16[2048,3,128]{0,2,1:T(8,128)(2,1)}, u32[]{:S(2)}) copy-start(bf16[2048,3,128]{0,2,1:T(8,128)(2,1)} %copy.32) | copy-start | bytes 4718596
  35.0 17.7 %collective-permute-start.6 = (bf16[32,2048]{1,0:T(8,128)(2,1)S(1)}, bf16[32,2048]{1,0:T(8,128)(2,1)S(1)}, u32[]{:S(2)}, u32[]{:S(2)}) collective-permute-start(bf16[32,2048]{1,0:T(8,128)(2,1)S(1)} %slice.44), channel_id=1, source_target_pairs={{0,64},{32,96},{64,128},{96,160},{128,192},{160,224},{192,0},{224,... | collective-permute-start | bytes 393224 | tf_op jit(solution)/shard_map/ppermute | solution.py:119
  36.1 16.5 %collective-permute-start.7 = (bf16[32,2048]{1,0:T(8,128)(2,1)S(1)}, bf16[32,2048]{1,0:T(8,128)(2,1)S(1)}, u32[]{:S(2)}, u32[]{:S(2)}) collective-permute-start(bf16[32,2048]{1,0:T(8,128)(2,1)S(1)} %slice.45), channel_id=1, source_target_pairs={{0,192},{32,224},{64,0},{96,32},{128,64},{160,96},{192,128},{224,1... | collective-permute-start | bytes 393224 | tf_op jit(solution)/shard_map/ppermute | solution.py:119
  40.2 12.5 %collective-permute-start.4 = (bf16[64,2048]{1,0:T(8,128)(2,1)}, bf16[64,2048]{1,0:T(8,128)(2,1)S(1)}, u32[]{:S(2)}, u32[]{:S(2)}) collective-permute-start(bf16[64,2048]{1,0:T(8,128)(2,1)} %collective-permute-done.2), channel_id=1, source_target_pairs={{0,32},{32,64},{64,96},{96,128},{128,160},{160,192},{192,224},{224... | collective-permute-start | bytes 786440 | tf_op jit(solution)/shard_map/ppermute | solution.py:119
  40.2 12.5 %collective-permute-start.5 = (bf16[64,2048]{1,0:T(8,128)(2,1)}, bf16[64,2048]{1,0:T(8,128)(2,1)S(1)}, u32[]{:S(2)}, u32[]{:S(2)}) collective-permute-start(bf16[64,2048]{1,0:T(8,128)(2,1)} %collective-permute-done.3), channel_id=1, source_target_pairs={{0,224},{32,0},{64,32},{96,64},{128,96},{160,128},{192,160},{224,1... | collective-permute-start | bytes 786440 | tf_op jit(solution)/shard_map/ppermute | solution.py:119
  68.2 7.9 %collective-permute-start.10 = (bf16[512,256]{1,0:T(8,128)(2,1)S(1)}, bf16[512,256]{1,0:T(8,128)(2,1)S(1)}, u32[]{:S(2)}, u32[]{:S(2)}) collective-permute-start(bf16[512,256]{1,0:T(8,128)(2,1)S(1)} %get-tuple-element.19), channel_id=1, source_target_pairs={{0,16},{1,5},{2,18},{3,7},{4,20},{5,1},{6,22},{7,3},{8,24},{9,13},... | collective-permute-start | bytes 786440 | tf_op jit(solution)/shard_map/ppermute | solution.py:93
  71.2 7.7 %collective-permute-start.8 = (bf16[512,256]{1,0:T(8,128)(2,1)S(1)}, bf16[512,256]{1,0:T(8,128)(2,1)S(1)}, u32[]{:S(2)}, u32[]{:S(2)}) collective-permute-start(bf16[512,256]{1,0:T(8,128)(2,1)S(1)} %get-tuple-element.19), channel_id=1, source_target_pairs={{0,8},{1,3},{2,10},{3,5},{4,12},{5,7},{6,14},{7,1},{8,16},{9,11},{... | collective-permute-start | bytes 786440 | tf_op jit(solution)/shard_map/ppermute | solution.py:93
  71.8 7.2 %collective-permute-start.9 = (bf16[512,256]{1,0:T(8,128)(2,1)S(1)}, bf16[512,256]{1,0:T(8,128)(2,1)S(1)}, u32[]{:S(2)}, u32[]{:S(2)}) collective-permute-start(bf16[512,256]{1,0:T(8,128)(2,1)S(1)} %get-tuple-element.19), channel_id=1, source_target_pairs={{0,24},{1,7},{2,26},{3,1},{4,28},{5,3},{6,30},{7,5},{8,0},{9,15},{... | collective-permute-start | bytes 786440 | tf_op jit(solution)/shard_map/ppermute | solution.py:93
  79.0 14.9 %collective-permute-start.11 = (bf16[2048,256]{1,0:T(8,128)(2,1)S(1)}, bf16[2048,256]{1,0:T(8,128)(2,1)S(1)}, u32[]{:S(2)}, u32[]{:S(2)}) collective-permute-start(bf16[2048,256]{1,0:T(8,128)(2,1)S(1)} %pad_maximum_fusion), channel_id=1, source_target_pairs={{0,2},{1,9},{2,4},{3,11},{4,6},{5,13},{6,0},{7,15},{8,10},{9,17},{... | collective-permute-start | bytes 3145736 | tf_op jit(solution)/shard_map/ppermute | solution.py:93
  80.7 14.8 %collective-permute-start.12 = (bf16[2048,256]{1,0:T(8,128)(2,1)S(1)}, bf16[2048,256]{1,0:T(8,128)(2,1)S(1)}, u32[]{:S(2)}, u32[]{:S(2)}) collective-permute-start(bf16[2048,256]{1,0:T(8,128)(2,1)S(1)} %pad_maximum_fusion), channel_id=1, source_target_pairs={{0,6},{1,25},{2,0},{3,27},{4,2},{5,29},{6,4},{7,31},{8,14},{9,1},{... | collective-permute-start | bytes 3145736 | tf_op jit(solution)/shard_map/ppermute | solution.py:93
  81.1 26.3 %collective-permute-start.13 = (bf16[2048,256]{1,0:T(8,128)(2,1)S(1)}, bf16[2048,256]{1,0:T(8,128)(2,1)S(1)}, u32[]{:S(2)}, u32[]{:S(2)}) collective-permute-start(bf16[2048,256]{1,0:T(8,128)(2,1)S(1)} %pad_maximum_fusion), channel_id=1, source_target_pairs={{0,4},{1,17},{2,6},{3,19},{4,0},{5,21},{6,2},{7,23},{8,12},{9,25},... | collective-permute-start | bytes 3145736 | tf_op jit(solution)/shard_map/ppermute | solution.py:93
  108.5 14.1 %collective-permute-start.14 = (bf16[8192,256]{1,0:T(8,128)(2,1)}, bf16[8192,256]{1,0:T(8,128)(2,1)}, u32[]{:S(2)}, u32[]{:S(2)}) collective-permute-start(bf16[8192,256]{1,0:T(8,128)(2,1)} %constant_dynamic-update-slice_fusion.keyval_ref), channel_id=1, source_target_pairs={{0,1},{1,0},{2,3},{3,2},{4,5},{5,4},{6,7},{7,6},{8,9},{9,8},{10,11... | collective-permute-start | bytes 12582920 | tf_op jit(solution)/shard_map/ppermute | solution.py:114
  122.5 19.9 %copy-start.9 = (s32[64,6]{0,1:T(8,128)S(1)}, s32[64,6]{0,1:T(8,128)}, u32[]{:S(2)}) copy-start(s32[64,6]{0,1:T(8,128)} %param.19) | copy-start | bytes 4612
  136.2 16.0 %all-to-all-start = ((bf16[8,64,128]{2,1,0:T(8,128)(2,1)}), bf16[8,64,128]{2,1,0:T(8,128)(2,1)S(1)}, u32[]{:S(2)}, u32[]{:S(2)}) async-start(bf16[8,64,128]{2,1,0:T(8,128)(2,1)} %bitcast.6), calls=%async_computation | async-start | bytes 262144 | tf_op jit(solution)/shard_map/all_to_all | solution.py:198
  152.2 3.0 copy-start.5
  152.2 3.9 %copy-start.8 = (f32[2048]{0:T(1024)S(1)}, f32[2048]{0:T(1024)}, u32[]{:S(2)}) copy-start(f32[2048]{0:T(1024)} %param.24) | copy-start | bytes 24580
  156.1 1.3 copy-start.2
  156.1 60.2 %slice-start = ((s8[6291456]{0:T(1024)(128)(4,1)}), s8[4194304]{0:T(1024)(128)(4,1)S(1)}, s32[]{:S(2)}) async-start(s8[6291456]{0:T(1024)(128)(4,1)} %bitcast.141), calls=%async_computation.4 | async-start | bytes 8388608
  157.4 58.8 %slice-start.1 = ((s8[6291456]{0:T(1024)(128)(4,1)}), s8[2097152]{0:T(1024)(128)(4,1)S(1)}, s32[]{:S(2)}) async-start(s8[6291456]{0:T(1024)(128)(4,1)} %bitcast.141), calls=%async_computation.5 | async-start | bytes 4194304
  214.2 2.0 copy-start.6
  233.7 6.2 %copy-start.7 = (bf16[2048,32]{0,1:T(8,128)(2,1)S(1)}, bf16[2048,32]{0,1:T(8,128)(2,1)}, u32[]{:S(2)}) copy-start(bf16[2048,32]{0,1:T(8,128)(2,1)} %param.25) | copy-start | bytes 393220
  233.7 60.7 %all-to-all-start.2 = ((bf16[32,32,2048]{2,1,0:T(8,128)(2,1)}), bf16[32,32,2048]{2,1,0:T(8,128)(2,1)}, u32[]{:S(2)}, u32[]{:S(2)}) async-start(bf16[32,32,2048]{2,1,0:T(8,128)(2,1)} %convolution_convert_fusion), calls=%async_computation.2 | async-start | bytes 8388608 | tf_op jit(solution)/shard_map/all_to_all | solution.py:239
  294.4 3.2 %copy-start.3 = (f32[64,2048]{1,0:T(8,128)S(1)}, f32[64,2048]{1,0:T(8,128)}, u32[]{:S(2)}) copy-start(f32[64,2048]{1,0:T(8,128)} %copy-done.2) | copy-start | bytes 1572868
Sparse Core Ops, SparseCore 0:
  66.6 55.4 all-gather.1
